TPU v7x, 32 devices: a whole 2x2x4 slice. The times are simulated.
32 devices in a mesh: grp: 2 (over y), vec: 4 (over z), walk: 2 (over x), orb: 2 (over core).
Axes of the slice: x: 2, y: 2, z: 4, core: 2. Of those that a mesh axis runs over, the one named last changes fastest.
Arguments:
- walkers: bfloat16 [32, 512, 128], P(('grp', 'walk'), 'orb'), parts along dimension 0, may hold values from -3 to 3
- inv_intersection: bfloat16 [32, 128, 128], P(('grp', 'walk')), parts along dimension 0, may hold values from -0.5 to 0.5
- trial: bfloat16 [512, 128], replicated, may hold values from -0.25 to 0.25
- vectors: bfloat16 [32, 512, 512], P('vec', 'orb')
- aux_field: float32 [32, 32], P(('grp', 'walk'), 'vec'), parts along dimension 0, may hold values from -5 to 5
- log_weight: float32 [32], P(('grp', 'walk')), parts along dimension 0, may hold values from -4 to 4
- copy_list: int32 [32], P(('grp', 'walk')), parts along dimension 0, may hold values from 0 to 15
Outputs:
- walkers_out: bfloat16 [32, 512, 128], P(('grp', 'walk'), 'orb'), parts along dimension 0
- weights_out: float32 [32], P(('grp', 'walk')), parts along dimension 0
There are 2 independent parts, one for each index of `grp`. A program takes and returns all parts, laid end to end along the dimension named above; an argument that names none is the same for every part. Nothing has to cross between parts.
Inputs may be any that keep to these rules, and one draw needn't show every extreme that they name: `copy_list`: the walker, within the same ensemble, whose copy fills the slot.
All inputs are finite; a program needn't handle non-finite values.
Results may differ from a plain program's by a relative error of at most 0.008.
Values may be sent and summed in bfloat16 or wider, within the bound.
No kernel may reach another device: no remote copies, remote signals or barrier semaphores. Data moves between devices by JAX's collectives and lax.ppermute only.
A program may use at most 64 MiB of HBM per device.

v0:
```python
from functools import partial
import math
import jax
import jax.numpy as jnp
from jax import lax
from jax.sharding import PartitionSpec as P

ORDER = 6
step_root = math.sqrt(0.08)


def fold_rows(operator, carry, piece, start):
    return jnp.einsum("wnm,wme->wne", operator, piece, preferred_element_type=jnp.float32)


def per_device(walkers, inv_intersection, trial, vectors, aux_field, log_weight, copy_list):
    green = jnp.einsum(
        "wne,wef->wnf", walkers, inv_intersection, preferred_element_type=jnp.float32
    ).astype(jnp.bfloat16)
    mixed = jnp.einsum("gnm,me->gne", vectors, trial, preferred_element_type=jnp.float32).astype(
        jnp.bfloat16
    )
    partial_bias = jnp.einsum("wne,gne->wg", green, mixed, preferred_element_type=jnp.float32)
    bias = lax.psum(partial_bias, "orb")
    shift = -step_root * bias
    field = aux_field - shift
    own_factor = jnp.sum(aux_field * shift - 0.5 * shift * shift, axis=1)
    new_log = log_weight + lax.psum(own_factor, "vec")
    weighted = (field * step_root).astype(jnp.bfloat16)
    local_operator = jnp.einsum(
        "wg,gnm->wnm", weighted, vectors, preferred_element_type=jnp.float32
    )
    operator = lax.psum(local_operator, "vec").astype(jnp.bfloat16)
    running = walkers.astype(jnp.float32)
    folder = partial(fold_rows, operator)
    operand = walkers
    for degree in range(1, ORDER + 1):
        initial = jnp.zeros(running.shape, jnp.float32)
        summed = folder(initial, lax.all_gather(operand, "orb", axis=1, tiled=True), jnp.int32(0))
        new_term = (summed / degree).astype(jnp.bfloat16)
        running = running + new_term.astype(jnp.float32)
        if degree < ORDER:
            operand = new_term
    propagated = running.astype(jnp.bfloat16)
    every_walker = lax.all_gather(propagated, "walk", axis=0, tiled=True)
    every_log = lax.all_gather(new_log, "walk", axis=0, tiled=True)
    return (every_walker[copy_list], every_log[copy_list])


def solution(mesh):
    return jax.shard_map(
        per_device,
        mesh=mesh,
        in_specs=(
            P(("grp", "walk"), "orb", None),
            P(("grp", "walk"), None, None),
            P(),
            P("vec", "orb", None),
            P(("grp", "walk"), "vec"),
            P(("grp", "walk")),
            P(("grp", "walk")),
        ),
        out_specs=(P(("grp", "walk"), "orb", None), P(("grp", "walk"))),
        check_vma=False,
    )
```

profile of v0, /device:TPU:0, one launch (start us, length us, event | category | flops | bytes accessed | tf_op | source)
XLA Modules:
  0.0 276.8 jit_solution(15812537913773210420)
XLA Ops:
  7.2 0.7 all-gather.8.cloned.1.call-update
  8.0 1.4 convolution_convert_fusion.1
  9.4 0.4 copy.23
  9.8 1.5 convolution_convert_fusion.2
  11.3 1.4 copy.24
  12.7 0.4 convolution_bitcast_fusion
  13.2 2.6 psum.21
  15.8 3.3 %fusion = f32[8,256,512]{2,0,1:T(8,128)} fusion(bf16[8,256,512]{2,1,0:T(8,128)(2,1)S(1)} %copy-done, f32[8,8]{1,0:T(8,128)S(1)} %copy-done.4, f32[8,8]{1,0:T(8,128)S(1)} %psum.21), kind=kOutput, calls=%fused_computation.2 | convolution fusion | flops 16777472 | bytes 6291968 | tf_op jit(solution)/shard_map/wg,gnm->wnm/dot_general | solution.py:30
  19.1 0.1 subtract_reduce_fusion
  19.2 150.7 %all-reduce.3 = (bf16[8,256,512]{2,0,1:T(8,128)(2,1)}, f32[8]{0:T(128)S(1)}) all-reduce(f32[8,256,512]{2,0,1:T(8,128)} %fusion, f32[8]{0:T(128)S(1)} %subtract_reduce_fusion), channel_id=1, replica_groups=mesh['grp'=2,'vec'=4,'walk'=2,'orb'=2] {'vec'}, use_global_device_ids=true, to_apply=%region_1.0 | all-reduce | flops 1048584 | bytes 6291520 | tf_op jit(solution)/shard_map/psum | solution.py:33
  169.9 4.0 %convolution_convert_fusion = bf16[8,256,128]{2,1,0:T(8,128)(2,1)} fusion(bf16[8,512,128]{2,1,0:T(8,128)(2,1)} %all-gather.8.cloned.1.call-done, bf16[8,256,512]{2,0,1:T(8,128)(2,1)} %get-tuple-element.2), kind=kOutput, calls=%fused_computation.9 | convolution fusion | flops 268697600 | bytes 3670016 | tf_op jit(solution)/shard_map/wnm,wme->wne/dot_general | solution.py:13
  173.9 0.0 all-gather.12.cloned.1.call-start
  173.9 8.3 %all-gather.10.cloned.1.call-done = bf16[8,512,128]{2,1,0:T(8,128)(2,1)} async-done(((bf16[8,256,128]{2,1,0:T(8,128)(2,1)}), bf16[8,512,128]{2,1,0:T(8,128)(2,1)}) %all-gather.10.cloned.1.call-update) | async-done | bytes 1048592 | tf_op jit(solution)/shard_map/all_gather | solution.py:39
  182.2 4.1 %fusion.2 = bf16[8,256,128]{2,1,0:T(8,128)(2,1)} fusion(bf16[8,512,128]{2,1,0:T(8,128)(2,1)} %all-gather.10.cloned.1.call-done, bf16[8,256,512]{2,0,1:T(8,128)(2,1)} %get-tuple-element.2), kind=kOutput, calls=%fused_computation.11 | convolution fusion | flops 268959744 | bytes 3670016 | tf_op jit(solution)/shard_map/wnm,wme->wne/dot_general | solution.py:13
  186.3 0.0 all-gather.14.cloned.1.call-start
  186.4 10.3 %all-gather.12.cloned.1.call-done = bf16[8,512,128]{2,1,0:T(8,128)(2,1)} async-done(((bf16[8,256,128]{2,1,0:T(8,128)(2,1)}), bf16[8,512,128]{2,1,0:T(8,128)(2,1)}) %all-gather.12.cloned.1.call-update) | async-done | bytes 1048592 | tf_op jit(solution)/shard_map/all_gather | solution.py:39
  196.7 4.1 %fusion.3 = bf16[8,256,128]{2,1,0:T(8,128)(2,1)} fusion(bf16[8,512,128]{2,1,0:T(8,128)(2,1)} %all-gather.12.cloned.1.call-done, bf16[8,256,512]{2,0,1:T(8,128)(2,1)} %get-tuple-element.2), kind=kOutput, calls=%fused_computation.12 | convolution fusion | flops 268959744 | bytes 3670016 | tf_op jit(solution)/shard_map/wnm,wme->wne/dot_general | solution.py:13
  200.7 0.0 all-gather.16.cloned.1.call-start
  200.8 10.3 %all-gather.14.cloned.1.call-done = bf16[8,512,128]{2,1,0:T(8,128)(2,1)} async-done(((bf16[8,256,128]{2,1,0:T(8,128)(2,1)}), bf16[8,512,128]{2,1,0:T(8,128)(2,1)}) %all-gather.14.cloned.1.call-update) | async-done | bytes 1048592 | tf_op jit(solution)/shard_map/all_gather | solution.py:39
  211.1 4.0 %fusion.4 = bf16[8,256,128]{2,1,0:T(8,128)(2,1)} fusion(bf16[8,512,128]{2,1,0:T(8,128)(2,1)} %all-gather.14.cloned.1.call-done, bf16[8,256,512]{2,0,1:T(8,128)(2,1)} %get-tuple-element.2), kind=kOutput, calls=%fused_computation.13 | convolution fusion | flops 268959744 | bytes 3670016 | tf_op jit(solution)/shard_map/wnm,wme->wne/dot_general | solution.py:13
  215.2 0.0 all-gather.18.cloned.1.call-start
  215.2 10.3 %all-gather.16.cloned.1.call-done = bf16[8,512,128]{2,1,0:T(8,128)(2,1)} async-done(((bf16[8,256,128]{2,1,0:T(8,128)(2,1)}), bf16[8,512,128]{2,1,0:T(8,128)(2,1)}) %all-gather.16.cloned.1.call-update) | async-done | bytes 1048592 | tf_op jit(solution)/shard_map/all_gather | solution.py:39
  225.5 4.0 %fusion.5 = bf16[8,256,128]{2,1,0:T(8,128)(2,1)} fusion(bf16[8,512,128]{2,1,0:T(8,128)(2,1)} %all-gather.16.cloned.1.call-done, bf16[8,256,512]{2,0,1:T(8,128)(2,1)} %get-tuple-element.2), kind=kOutput, calls=%fused_computation.14 | convolution fusion | flops 268959744 | bytes 3670016 | tf_op jit(solution)/shard_map/wnm,wme->wne/dot_general | solution.py:13
  229.6 0.0 all-gather.20.cloned.1.call-start
  229.7 10.3 %all-gather.18.cloned.1.call-done = bf16[8,512,128]{2,1,0:T(8,128)(2,1)} async-done(((bf16[8,256,128]{2,1,0:T(8,128)(2,1)}), bf16[8,512,128]{2,1,0:T(8,128)(2,1)}) %all-gather.18.cloned.1.call-update) | async-done | bytes 1048592 | tf_op jit(solution)/shard_map/all_gather | solution.py:39
  239.9 4.7 %fusion.9 = bf16[8,256,128]{2,1,0:T(8,128)(2,1)} fusion(bf16[8,512,128]{2,1,0:T(8,128)(2,1)} %all-gather.18.cloned.1.call-done, bf16[8,256,128]{2,1,0:T(8,128)(2,1)} %fusion.5, bf16[8,256,128]{2,1,0:T(8,128)(2,1)} %fusion.4, bf16[8,256,128]{2,1,0:T(8,128)(2,1)} %fusion.3, bf16[8,256,128]{2,1,0:T(8,128)(2,1)} %fusion.2, ...), kind=kOutput, calls=%fused_computation.18 | convolution fusion | flops 272629760 | bytes 6815744 | tf_op jit(solution)/shard_map/wnm,wme->wne/dot_general | solution.py:13
  244.7 0.6 dynamic-slice
  246.0 0.1 add_dynamic-update-slice_fusion
  246.1 4.9 %all-reduce = f32[16]{0:T(128)S(1)} all-reduce(f32[16]{0:T(128)S(1)} %add_dynamic-update-slice_fusion), channel_id=1, replica_groups=mesh['grp'=2,'vec'=4,'walk'=2,'orb'=2] {'walk'}, use_global_device_ids=true, to_apply=%add | all-reduce | flops 16 | bytes 128
  251.0 1.2 gather_fusion.1
  252.2 15.2 %all-gather.20.cloned.1.call-done = bf16[16,256,128]{2,1,0:T(8,128)(2,1)} async-done(((bf16[8,256,128]{2,1,0:T(8,128)(2,1)}), bf16[16,256,128]{2,1,0:T(8,128)(2,1)}) %all-gather.20.cloned.1.call-update) | async-done | bytes 1048592 | tf_op jit(solution)/shard_map/all_gather | solution.py:45
  267.3 2.6 gather_fusion
  (28 shorter events, 0.2 us)
Async XLA Ops:
  7.2 2.6 copy-start
  7.2 2.6 copy-start.3
  7.2 162.7 %all-gather.8.cloned.1.call-start = ((), (), s32[]{:S(2)}) async-start(), calls=%async_computation | async-start | bytes 1572864 | tf_op jit(solution)/shard_map/all_gather | solution.py:39
  7.9 174.3 %all-gather.10.cloned.1.call-start = ((), (), s32[]{:S(2)}) async-start(), calls=%async_computation.1 | async-start | bytes 1572864 | tf_op jit(solution)/shard_map/all_gather | solution.py:39
  9.8 6.0 %copy-start.4 = (f32[8,8]{1,0:T(8,128)S(1)}, f32[8,8]{1,0:T(8,128)}, u32[]{:S(2)}) copy-start(f32[8,8]{1,0:T(8,128)} %param.11) | copy-start | bytes 772
  173.9 22.8 %all-gather.12.cloned.1.call-start = ((), (), s32[]{:S(2)}) async-start(), calls=%async_computation.2 | async-start | bytes 1572864 | tf_op jit(solution)/shard_map/all_gather | solution.py:39
  186.3 24.8 %all-gather.14.cloned.1.call-start = ((), (), s32[]{:S(2)}) async-start(), calls=%async_computation.3 | async-start | bytes 1572864 | tf_op jit(solution)/shard_map/all_gather | solution.py:39
  200.7 24.8 %all-gather.16.cloned.1.call-start = ((), (), s32[]{:S(2)}) async-start(), calls=%async_computation.4 | async-start | bytes 1572864 | tf_op jit(solution)/shard_map/all_gather | solution.py:39
  215.2 24.8 %copy-start.1 = (bf16[8,256,128]{2,1,0:T(8,128)(2,1)S(1)}, bf16[8,256,128]{2,1,0:T(8,128)(2,1)}, u32[]{:S(2)}) copy-start(bf16[8,256,128]{2,1,0:T(8,128)(2,1)} %param.7) | copy-start | bytes 1572868
  215.2 24.8 %copy-start.2 = (bf16[8,256,128]{2,1,0:T(8,128)(2,1)S(1)}, bf16[8,256,128]{2,1,0:T(8,128)(2,1)}, u32[]{:S(2)}) copy-start(bf16[8,256,128]{2,1,0:T(8,128)(2,1)} %convolution_convert_fusion) | copy-start | bytes 1572868
  215.2 24.8 %all-gather.18.cloned.1.call-start = ((), (), s32[]{:S(2)}) async-start(), calls=%async_computation.5 | async-start | bytes 1572864 | tf_op jit(solution)/shard_map/all_gather | solution.py:39
  229.6 15.1 %copy-start.7 = (u32[32]{0:T(128)S(1)}, u32[32]{0:T(128)}, u32[]{:S(2)}) copy-start(u32[32]{0:T(128)} %constant.31) | copy-start | bytes 388
  229.6 16.4 %copy-start.5 = (f32[8]{0:T(128)S(1)}, f32[8]{0:T(128)}, u32[]{:S(2)}) copy-start(f32[8]{0:T(128)} %param.12) | copy-start | bytes 100
  229.6 21.4 %copy-start.6 = (s32[8]{0:T(128)S(1)}, s32[8]{0:T(128)}, u32[]{:S(2)}) copy-start(s32[8]{0:T(128)} %param.13) | copy-start | bytes 100
  229.6 37.7 %all-gather.20.cloned.1.call-start = ((), (), s32[]{:S(2)}) async-start(), calls=%async_computation.6 | async-start | bytes 1572864 | tf_op jit(solution)/shard_map/all_gather | solution.py:45
Sparse Core Ops, SparseCore 0:
  9.5 11.7 all-gather.7
  174.0 8.1 all-gather.9
  186.4 10.1 all-gather.11
  200.9 10.1 all-gather.13
  215.3 10.1 all-gather.15
  229.7 10.1 all-gather.17
  244.8 22.4 all-gather.19
where the time goes:
time: 277 us
  blocking collectives  158 us (57%)
  waiting for transfers between devices  65.4 us (24%)
  matrix products  31.5 us (11%)
  between operations  14.9 us (5%)
  local copies, waits for them, and re-layouts  6.25 us (2%)
    psum x1, blocking collectives, per_device(): operator = lax.psum(local_operator, 'vec').astype(jnp.bfloat16)  151 us
    all_gather x6, waiting for transfers between devices, per_device(): lax.all_gather(operand, 'orb', axis=1, tiled=True)  49.4 us
    dot_general x6, matrix products, fold_rows(): jnp.einsum('wnm,wme->wne', operator, piece, preferred_element_type=jnp.fl...  24.9 us
    all_gather x1, waiting for transfers between devices, per_device(): every_walker = lax.all_gather(propagated, 'walk', axis=0, tiled=True)  15.2 us
  transfers between devices with their start and end apart: 7, of which 6 were waited for; matrix products, arithmetic and copies ran while one was open for 4% of the time, Pallas kernels for 0%

commit v1 on v0

--- a/solution.py
+++ b/solution.py
@@ -7,6 +7,11 @@
 
 ORDER = 6
 step_root = math.sqrt(0.08)
+
+
+def all_by_exchange(shard, axis, dim):
+    stack = jnp.stack([shard] * lax.axis_size(axis))
+    return jnp.concatenate(lax.all_to_all(stack, axis, 0, 0), axis=dim)
 
 
 def fold_rows(operator, carry, piece, start):
@@ -36,7 +41,7 @@
     operand = walkers
     for degree in range(1, ORDER + 1):
         initial = jnp.zeros(running.shape, jnp.float32)
-        summed = folder(initial, lax.all_gather(operand, "orb", axis=1, tiled=True), jnp.int32(0))
+        summed = folder(initial, all_by_exchange(operand, "orb", 1), jnp.int32(0))
         new_term = (summed / degree).astype(jnp.bfloat16)
         running = running + new_term.astype(jnp.float32)
         if degree < ORDER:

time: 277 us -> 248 us (0.90)
  waiting for transfers between devices: 65.4 us -> 12.2 us
  blocking collectives: 158 us -> 183 us
  matrix products: 31.5 us -> 19.7 us
  local copies, waits for them, and re-layouts: 6.25 us -> 10.3 us
  starting transfers between devices: 0.29 us -> 3.75 us
  other arithmetic: 0.23 us -> 3.1 us
    all_gather x6 -> x0, waiting for transfers between devices: 49.4 us -> none  [per_device(): lax.all_gather(operand, 'orb', axis=1, tiled=True)]
    all_to_all x0 -> x5, blocking collectives: none -> 23.1 us  [all_by_exchange(): return jnp.concatenate(lax.all_to_all(stack, axis, 0, 0), axis=dim)]
    dot_general x6, matrix products: 24.9 us -> 11.2 us  [fold_rows(): jnp.einsum('wnm,wme->wne', operator, piece, preferred_element_type=jnp.fl...]
    all_to_all x0 -> x1, starting transfers between devices: none -> 3.71 us  [all_by_exchange(): return jnp.concatenate(lax.all_to_all(stack, axis, 0, 0), axis=dim)]
    all_gather x1, waiting for transfers between devices: 15.2 us -> 12.2 us  [per_device(): every_walker = lax.all_gather(propagated, 'walk', axis=0, tiled=True)]
    another operation x0 -> x6, other arithmetic: none -> 2.87 us  [all_by_exchange(): stack = jnp.stack([shard] * lax.axis_size(axis))]
  transfers between devices with their start and end apart: 7 -> 2, of which waited for: 6 -> 1; matrix products, arithmetic and copies ran while one was open for 4% -> 6% of each run, Pallas kernels for 0% -> 0%
where the time goes in v1:
time: 248 us; the launch traced here: 247 us
  blocking collectives  183 us (74%)
  matrix products  19.7 us (8%)
  between operations  14.9 us (6%)
  waiting for transfers between devices  12.2 us (5%)
  local copies, waits for them, and re-layouts  10.3 us (4%)
  starting transfers between devices  3.75 us (2%)
  other arithmetic  3.1 us (1%)
    psum x1, blocking collectives, per_device(): operator = lax.psum(local_operator, 'vec').astype(jnp.bfloat16)  152 us
    all_to_all x5, blocking collectives, all_by_exchange(): return jnp.concatenate(lax.all_to_all(stack, axis, 0, 0), axis=dim)  23.1 us
    all_gather x1, waiting for transfers between devices, per_device(): every_walker = lax.all_gather(propagated, 'walk', axis=0, tiled=True)  12.2 us
    dot_general x6, matrix products, fold_rows(): jnp.einsum('wnm,wme->wne', operator, piece, preferred_element_type=jnp.fl...  11.2 us
  transfers between devices with their start and end apart: 2, of which 1 were waited for; matrix products, arithmetic and copies ran while one was open for 6% of the time, Pallas kernels for 0%

profile of v1, /device:TPU:0, one launch (start us, length us, event | category | flops | bytes accessed | tf_op | source)
XLA Modules:
  0.0 246.9 jit_solution(15519430494715761669)
XLA Ops:
  7.2 2.4 pad_maximum_fusion
  9.6 3.7 %all-to-all-start = ((bf16[2,8,256,128]{3,2,1,0:T(8,128)(2,1)}), bf16[2,8,256,128]{3,2,1,0:T(8,128)(2,1)S(1)}, u32[]{:S(2)}, u32[]{:S(2)}) async-start(bf16[2,8,256,128]{3,2,1,0:T(8,128)(2,1)} %pad_maximum_fusion), calls=%async_computation | async-start | bytes 2097152 | tf_op jit(solution)/shard_map/all_to_all | solution.py:14
  13.4 2.1 convolution_convert_fusion.1
  15.5 2.2 copy.30
  17.8 1.5 convolution_convert_fusion.2
  19.3 2.2 copy.31
  21.5 1.6 convolution_bitcast_fusion
  23.1 2.6 %psum.21 = f32[8,8]{1,0:T(8,128)S(1)} all-reduce(f32[8,8]{1,0:T(8,128)S(1)} %convolution_bitcast_fusion), channel_id=1, replica_groups=mesh['grp'=2,'vec'=4,'walk'=2,'orb'=2] {'orb'}, use_global_device_ids=true, to_apply=%region_0.0 | all-reduce | flops 64 | bytes 512 | tf_op jit(solution)/shard_map/psum | solution.py:29
  25.7 3.2 %fusion = f32[8,256,512]{2,0,1:T(8,128)} fusion(bf16[8,256,512]{2,1,0:T(8,128)(2,1)S(1)} %copy-done, f32[8,8]{1,0:T(8,128)S(1)} %copy-done.5, f32[8,8]{1,0:T(8,128)S(1)} %psum.21), kind=kOutput, calls=%fused_computation.2 | convolution fusion | flops 16777472 | bytes 6291968 | tf_op jit(solution)/shard_map/wg,gnm->wnm/dot_general | solution.py:35
  29.0 0.1 subtract_reduce_fusion
  29.1 1.1 copy.33
  30.2 152.2 %all-reduce.3 = (bf16[8,256,512]{2,0,1:T(8,128)(2,1)}, f32[8]{0:T(128)S(1)}) all-reduce(f32[8,256,512]{2,0,1:T(8,128)} %fusion, f32[8]{0:T(128)S(1)} %subtract_reduce_fusion), channel_id=1, replica_groups=mesh['grp'=2,'vec'=4,'walk'=2,'orb'=2] {'vec'}, use_global_device_ids=true, to_apply=%region_1.0 | all-reduce | flops 1048584 | bytes 6291520 | tf_op jit(solution)/shard_map/psum | solution.py:38
  182.4 2.9 %convolution_convert_fusion = bf16[8,256,128]{2,1,0:T(8,128)(2,1)S(1)} fusion(bf16[8,512,128]{2,1,0:T(8,128)(2,1)S(1)} %bitcast.46, bf16[8,256,512]{2,0,1:T(8,128)(2,1)} %get-tuple-element.2), kind=kOutput, calls=%fused_computation.9 | convolution fusion | flops 268697600 | bytes 3670016 | tf_op jit(solution)/shard_map/wnm,wme->wne/dot_general | solution.py:18
  185.3 0.1 pad_maximum_fusion.1
  185.4 4.7 %all_to_all.30 = bf16[2,8,256,128]{3,2,1,0:T(8,128)(2,1)S(1)} all-to-all(bf16[2,8,256,128]{3,2,1,0:T(8,128)(2,1)S(1)} %pad_maximum_fusion.1), channel_id=1, replica_groups=mesh['grp'=2,'vec'=4,'walk'=2,'orb'=2] {'orb'}, dimensions={0} | all-to-all | bytes 2097152 | tf_op jit(solution)/shard_map/all_to_all | solution.py:14
  190.2 1.5 fusion.2
  191.7 0.1 pad_maximum_fusion.2
  191.8 4.6 %all_to_all.31 = bf16[2,8,256,128]{3,2,1,0:T(8,128)(2,1)S(1)} all-to-all(bf16[2,8,256,128]{3,2,1,0:T(8,128)(2,1)S(1)} %pad_maximum_fusion.2), channel_id=1, replica_groups=mesh['grp'=2,'vec'=4,'walk'=2,'orb'=2] {'orb'}, dimensions={0} | all-to-all | bytes 2097152 | tf_op jit(solution)/shard_map/all_to_all | solution.py:14
  196.5 1.5 fusion.3
  198.1 4.6 %all_to_all.32 = bf16[2,8,256,128]{3,2,1,0:T(8,128)(2,1)S(1)} all-to-all(bf16[2,8,256,128]{3,2,1,0:T(8,128)(2,1)S(1)} %pad_maximum_fusion.3), channel_id=1, replica_groups=mesh['grp'=2,'vec'=4,'walk'=2,'orb'=2] {'orb'}, dimensions={0} | all-to-all | bytes 2097152 | tf_op jit(solution)/shard_map/all_to_all | solution.py:14
  202.7 1.5 fusion.4
  204.3 4.6 %all_to_all.33 = bf16[2,8,256,128]{3,2,1,0:T(8,128)(2,1)S(1)} all-to-all(bf16[2,8,256,128]{3,2,1,0:T(8,128)(2,1)S(1)} %pad_maximum_fusion.4), channel_id=1, replica_groups=mesh['grp'=2,'vec'=4,'walk'=2,'orb'=2] {'orb'}, dimensions={0} | all-to-all | bytes 2097152 | tf_op jit(solution)/shard_map/all_to_all | solution.py:14
  209.0 1.5 fusion.5
  210.5 0.1 pad_maximum_fusion.5
  210.6 4.7 %all_to_all.34 = bf16[2,8,256,128]{3,2,1,0:T(8,128)(2,1)S(1)} all-to-all(bf16[2,8,256,128]{3,2,1,0:T(8,128)(2,1)S(1)} %pad_maximum_fusion.5), channel_id=1, replica_groups=mesh['grp'=2,'vec'=4,'walk'=2,'orb'=2] {'orb'}, dimensions={0} | all-to-all | bytes 2097152 | tf_op jit(solution)/shard_map/all_to_all | solution.py:14
  215.4 2.3 fusion.9
  217.7 0.6 dynamic-slice
  219.0 0.1 add_dynamic-update-slice_fusion
  219.1 4.9 %all-reduce = f32[16]{0:T(128)S(1)} all-reduce(f32[16]{0:T(128)S(1)} %add_dynamic-update-slice_fusion), channel_id=1, replica_groups=mesh['grp'=2,'vec'=4,'walk'=2,'orb'=2] {'walk'}, use_global_device_ids=true, to_apply=%add | all-reduce | flops 16 | bytes 128
  224.0 1.2 gather_fusion.1
  225.2 12.2 %all-gather.2.cloned.1.call-done = bf16[16,256,128]{2,1,0:T(8,128)(2,1)} async-done(((bf16[8,256,128]{2,1,0:T(8,128)(2,1)}), bf16[16,256,128]{2,1,0:T(8,128)(2,1)}) %all-gather.2.cloned.1.call-update) | async-done | bytes 1048592 | tf_op jit(solution)/shard_map/all_gather | solution.py:50
  237.4 2.6 %gather_fusion = bf16[8,256,128]{2,1,0:T(8,128)(2,1)} fusion(bf16[16,256,128]{2,1,0:T(8,128)(2,1)} %all-gather.2.cloned.1.call-done, s32[1024]{0:T(1024)S(1)} %pad_clamp_fusion), kind=kCustom, calls=%fused_computation | custom fusion | bytes 1048608 | tf_op jit(solution)/shard_map/gather | solution.py:52
  (33 shorter events, 0.7 us)
Async XLA Ops:
  7.2 10.6 %copy-start = (bf16[8,256,512]{2,1,0:T(8,128)(2,1)S(1)}, bf16[8,256,512]{2,1,0:T(8,128)(2,1)}, u32[]{:S(2)}) copy-start(bf16[8,256,512]{2,1,0:T(8,128)(2,1)} %param.10) | copy-start | bytes 6291460
  7.2 6.2 %copy-start.3 = (bf16[8,128,128]{2,1,0:T(8,128)(2,1)S(1)}, bf16[8,128,128]{2,1,0:T(8,128)(2,1)}, u32[]{:S(2)}) copy-start(bf16[8,128,128]{2,1,0:T(8,128)(2,1)} %param.8) | copy-start | bytes 786436
  9.6 8.1 %copy-start.4 = (bf16[512,128]{1,0:T(8,128)(2,1)S(1)}, bf16[512,128]{1,0:T(8,128)(2,1)}, u32[]{:S(2)}) copy-start(bf16[512,128]{1,0:T(8,128)(2,1)} %param.9) | copy-start | bytes 393220
  9.6 19.5 %all-to-all-start = ((bf16[2,8,256,128]{3,2,1,0:T(8,128)(2,1)}), bf16[2,8,256,128]{3,2,1,0:T(8,128)(2,1)S(1)}, u32[]{:S(2)}, u32[]{:S(2)}) async-start(bf16[2,8,256,128]{3,2,1,0:T(8,128)(2,1)} %pad_maximum_fusion), calls=%async_computation | async-start | bytes 2097152 | tf_op jit(solution)/shard_map/all_to_all | solution.py:14
  13.3 224.0 %all-gather.2.cloned.1.call-start = ((), (), s32[]{:S(2)}) async-start(), calls=%async_computation.6 | async-start | bytes 1572864 | tf_op jit(solution)/shard_map/all_gather | solution.py:50
  17.8 8.0 %copy-start.5 = (f32[8,8]{1,0:T(8,128)S(1)}, f32[8,8]{1,0:T(8,128)}, u32[]{:S(2)}) copy-start(f32[8,8]{1,0:T(8,128)} %param.11) | copy-start | bytes 772
  30.2 152.2 %copy-start.2 = (bf16[8,2,256,128]{3,2,1,0:T(8,128)(2,1)S(1)}, bf16[8,2,256,128]{3,2,1,0:T(8,128)(2,1)}, u32[]{:S(2)}) copy-start(bf16[8,2,256,128]{3,2,1,0:T(8,128)(2,1)} %copy.33) | copy-start | bytes 3145732
  185.4 4.8 %copy-start.7 = (bf16[8,256,512]{2,0,1:T(8,128)(2,1)S(1)}, bf16[8,256,512]{2,0,1:T(8,128)(2,1)}, u32[]{:S(2)}) copy-start(bf16[8,256,512]{2,0,1:T(8,128)(2,1)} %get-tuple-element.2) | copy-start | bytes 6291460
  210.6 4.8 %copy-start.1 = (bf16[8,256,128]{2,1,0:T(8,128)(2,1)S(1)}, bf16[8,256,128]{2,1,0:T(8,128)(2,1)}, u32[]{:S(2)}) copy-start(bf16[8,256,128]{2,1,0:T(8,128)(2,1)} %param.7) | copy-start | bytes 1572868
  215.4 2.3 copy-start.9
  215.4 3.6 %copy-start.6 = (f32[8]{0:T(128)S(1)}, f32[8]{0:T(128)}, u32[]{:S(2)}) copy-start(f32[8]{0:T(128)} %param.12) | copy-start | bytes 100
  215.4 8.6 %copy-start.8 = (s32[8]{0:T(128)S(1)}, s32[8]{0:T(128)}, u32[]{:S(2)}) copy-start(s32[8]{0:T(128)} %param.13) | copy-start | bytes 100
Sparse Core Ops, SparseCore 0:
  217.8 19.5 all-gather.1
